TPU v7x, 32 devices: a whole 2x2x4 slice. The times are simulated.
32 devices in a mesh: img: 8 (over z, y), band: 4 (over x, core).
Axes of the slice: x: 2, y: 2, z: 4, core: 2. Of those that a mesh axis runs over, the one named last changes fastest.
Arguments:
- patches: bfloat16 [32, 576, 768], P('img', 'band'), may hold values from -6 to 6
- patch_mask: int32 [32, 576], P('img', 'band'), may hold values from 0 to 1, as said below
- band_first: int32 [32, 4], P('img'), may hold values from 0 to 18, as said below
- attn_gain: bfloat16 [768], replicated, may hold values from 0.5 to 1.5
- attn_shift: bfloat16 [768], replicated, may hold values from -3 to 3
- inproj_weight: bfloat16 [768, 2304], replicated, may hold values from -0.21875 to 0.21875
- inproj_bias: bfloat16 [2304], replicated, may hold values from -2 to 2
- rotary_freqs: bfloat16 [2, 12, 32], replicated, may hold values from -3 to 3
- outproj_weight: bfloat16 [768, 768], replicated, may hold values from -0.875 to 0.875
- outproj_bias: bfloat16 [768], replicated, may hold values from -2 to 2
- mlp_gain: bfloat16 [768], replicated, may hold values from 0.5 to 1.5
- mlp_shift: bfloat16 [768], replicated, may hold values from -3 to 3
- expand_weight: bfloat16 [768, 3072], replicated, may hold values from -0.21875 to 0.21875
- expand_bias: bfloat16 [3072], replicated, may hold values from -2 to 2
- reduce_weight: bfloat16 [3072, 768], replicated, may hold values from -0.109375 to 0.109375
- reduce_bias: bfloat16 [768], replicated, may hold values from -2 to 2
- cotangent: bfloat16 [32, 576, 768], P('img', 'band'), may hold values from -6 to 6
Outputs:
- block_out: bfloat16 [32, 576, 768], P('img', 'band')
- d_patches: bfloat16 [32, 576, 768], P('img', 'band')
- grad_attn_gain: float32 [768], P('img')
- grad_attn_shift: float32 [768], P('img')
- grad_inproj_weight: float32 [768, 2304], P('img')
- grad_inproj_bias: float32 [2304], P('img')
- grad_rotary_freqs: float32 [2, 12, 32], replicated
- grad_outproj_weight: float32 [768, 768], P('img')
- grad_outproj_bias: float32 [768], P('img')
- grad_mlp_gain: float32 [768], P('img')
- grad_mlp_shift: float32 [768], P('img')
- grad_expand_weight: float32 [768, 3072], P('img')
- grad_expand_bias: float32 [3072], P('img')
- grad_reduce_weight: float32 [3072, 768], P('img')
- grad_reduce_bias: float32 [768], P('img')
Inputs may be any that keep to these rules, and one draw needn't show every extreme that they name: `patch_mask`: each image has a square grid of side 24 * 7 // 12, 20 or 24, and image 0 has side 24; the grid's rows are split over the 4 bands as evenly as possible, earlier bands taking one row more; a slot of local row i and column j of band b is 1 exactly when i is under the band's row count and j under the side. `band_first`: the first patch row of each band of each image, consistent with patch_mask's row counts.
All inputs are finite; a program needn't handle non-finite values.
Results may differ from a plain program's by a relative error of at most 0.012.
The roundings to bfloat16 on the way count: a program that leaves them out, or rounds other values in their place, can miss the bound.
Values may be sent and summed in bfloat16 or wider, within the bound.
No kernel may reach another device: no remote copies, remote signals or barrier semaphores. Data moves between devices by JAX's collectives and lax.ppermute only.
A program may use at most 192 MiB of HBM per device.

v0:
```python
import jax
import jax.numpy as jnp
from jax import lax
from jax.sharding import PartitionSpec as P

GRID = 24
EPS = 1e-06
NEG = -1e30


def norm_parts(values):
    center = values - jnp.mean(values, -1, keepdims=True)
    rstd = lax.rsqrt(jnp.mean(center * center, -1, keepdims=True) + EPS)
    return (center * rstd, rstd)


def norm_back(grad, gain, xhat, rstd):
    scaled = grad * gain
    inner = jnp.mean(scaled * xhat, -1, keepdims=True)
    return rstd * (scaled - jnp.mean(scaled, -1, keepdims=True) - xhat * inner)


def turn(tensor, cosine, sine):
    half = tensor.shape[-1] // 2
    first, second = (tensor[..., :half], tensor[..., half:])
    return jnp.concatenate([first * cosine - second * sine, first * sine + second * cosine], -1)


def matrix_sum(grad):
    low = grad.astype(jnp.bfloat16)
    low = lax.psum_scatter(low, "band", scatter_dimension=1, tiled=True)
    low = lax.psum_scatter(low, "img", scatter_dimension=0, tiled=True)
    low = lax.all_gather(low, "band", axis=1, tiled=True)
    return low.astype(jnp.float32)


def local(
    patches,
    patch_mask,
    band_first,
    attn_gain,
    attn_shift,
    inproj_weight,
    inproj_bias,
    rotary_freqs,
    outproj_weight,
    outproj_bias,
    mlp_gain,
    mlp_shift,
    expand_weight,
    expand_bias,
    reduce_weight,
    reduce_bias,
    cotangent,
):
    single = jnp.float32
    low = jnp.bfloat16
    images, slots, width = patches.shape
    heads = rotary_freqs.shape[1]
    size = width // heads
    scale = size ** (-0.5)
    bands = lax.axis_size("band")
    here = lax.axis_index("band")

    def gather_image(values):
        return lax.all_to_all(values, "band", 0, 1, tiled=True)

    def spread_image(values):
        return lax.all_to_all(values, "band", 1, 0, tiled=True)

    patches = gather_image(patches)
    cotangent = gather_image(cotangent)
    mask = gather_image(patch_mask).astype(single)
    count = images // bands
    total = slots * bands
    starts = lax.dynamic_slice_in_dim(band_first, here * count, count, 0)
    row_in = jnp.arange(slots) // GRID
    rows = (starts[:, :, None] + row_in[None, None, :]).reshape(count, total).astype(single)
    cols = jnp.broadcast_to((jnp.arange(total) % GRID).astype(single)[None, :], rows.shape)
    freqs = rotary_freqs.astype(single)
    angles = rows[..., None, None] * freqs[0] + cols[..., None, None] * freqs[1]
    cosine, sine = (jnp.cos(angles), jnp.sin(angles))
    wide = patches.astype(single)
    xhat_one, rstd_one = norm_parts(wide)
    gain_one = attn_gain.astype(single)
    attn_in = (xhat_one * gain_one + attn_shift.astype(single)).astype(low)
    projected = jnp.dot(attn_in, inproj_weight, preferred_element_type=single)
    projected = projected + inproj_bias.astype(single)
    split = projected.reshape(count, total, 3, heads, size)
    query_rot = turn(split[:, :, 0], cosine, sine).astype(low)
    key_rot = turn(split[:, :, 1], cosine, sine).astype(low)
    value_low = split[:, :, 2].astype(low)
    scores = jnp.einsum("iqhd,ikhd->ihqk", query_rot, key_rot, preferred_element_type=single)
    masked = jnp.where(mask[:, None, None, :] > 0, scores * scale, NEG)
    expo = jnp.exp(masked - jnp.max(masked, -1, keepdims=True))
    probs = expo / jnp.sum(expo, -1, keepdims=True)
    probs_low = probs.astype(low)
    mix = jnp.einsum("ihqk,ikhd->iqhd", probs_low, value_low, preferred_element_type=single)
    mix = mix.reshape(count, total, width).astype(low)
    attn_out = jnp.dot(mix, outproj_weight, preferred_element_type=single)
    resid_mid = wide + attn_out + outproj_bias.astype(single)
    xhat_two, rstd_two = norm_parts(resid_mid)
    gain_two = mlp_gain.astype(single)
    mlp_in = (xhat_two * gain_two + mlp_shift.astype(single)).astype(low)
    pre_act = jnp.dot(mlp_in, expand_weight, preferred_element_type=single)
    pre_act = pre_act + expand_bias.astype(single)
    half_erf = 0.5 + 0.5 * lax.erf(pre_act * 0.5**0.5)
    hidden = (pre_act * half_erf).astype(low)
    slope = half_erf + pre_act * jnp.exp(-0.5 * pre_act * pre_act) * 0.3989422804014327
    branch = jnp.dot(hidden, reduce_weight, preferred_element_type=single)
    block_out = mask[..., None] * (resid_mid + branch + reduce_bias.astype(single))
    block_out = spread_image(block_out.astype(low))
    grad_top = cotangent.astype(single) * mask[..., None]
    grad_low = grad_top.astype(low)
    grad_reduce_weight = jnp.einsum("iqf,iqd->fd", hidden, grad_low, preferred_element_type=single)
    grad_reduce_bias = jnp.sum(grad_top, (0, 1))
    d_hidden = jnp.einsum("iqd,fd->iqf", grad_low, reduce_weight, preferred_element_type=single)
    d_pre = (d_hidden * slope).astype(low)
    grad_expand_weight = jnp.einsum("iqd,iqf->df", mlp_in, d_pre, preferred_element_type=single)
    grad_expand_bias = jnp.sum(d_pre.astype(single), (0, 1))
    d_mlp_in = jnp.einsum("iqf,df->iqd", d_pre, expand_weight, preferred_element_type=single)
    grad_mlp_gain = jnp.sum(d_mlp_in * xhat_two, (0, 1))
    grad_mlp_shift = jnp.sum(d_mlp_in, (0, 1))
    d_mid = grad_top + norm_back(d_mlp_in, gain_two, xhat_two, rstd_two)
    d_attn = d_mid.astype(low)
    grad_outproj_weight = jnp.einsum("iqe,iqd->ed", mix, d_attn, preferred_element_type=single)
    grad_outproj_bias = jnp.sum(d_attn.astype(single), (0, 1))
    d_mix = jnp.einsum("iqd,ed->iqe", d_attn, outproj_weight, preferred_element_type=single)
    d_mix = d_mix.astype(low).reshape(count, total, heads, size)
    d_values = jnp.einsum("ihqk,iqhd->ikhd", probs_low, d_mix, preferred_element_type=single)
    d_probs = jnp.einsum("iqhd,ikhd->ihqk", d_mix, value_low, preferred_element_type=single)
    inner = jnp.sum(probs * d_probs, -1, keepdims=True)
    d_scores = (probs * (d_probs - inner)).astype(low)
    d_qrot = scale * jnp.einsum("ihqk,ikhd->iqhd", d_scores, key_rot, preferred_element_type=single)
    d_krot = scale * jnp.einsum(
        "ihqk,iqhd->ikhd", d_scores, query_rot, preferred_element_type=single
    )
    half = size // 2
    slope_q = (
        d_qrot[..., half:] * query_rot[..., :half] - d_qrot[..., :half] * query_rot[..., half:]
    )
    slope_k = d_krot[..., half:] * key_rot[..., :half] - d_krot[..., :half] * key_rot[..., half:]
    d_angle = slope_q + slope_k
    grad_freqs = jnp.stack(
        [
            jnp.sum(rows[..., None, None] * d_angle, (0, 1)),
            jnp.sum(cols[..., None, None] * d_angle, (0, 1)),
        ]
    )
    d_queries = turn(d_qrot, cosine, -sine)
    d_keys = turn(d_krot, cosine, -sine)
    flat = (count, total, width)
    d_proj = jnp.concatenate(
        [d_queries.reshape(flat), d_keys.reshape(flat), d_values.reshape(flat)], -1
    ).astype(low)
    grad_inproj_weight = jnp.einsum("iqd,iqe->de", attn_in, d_proj, preferred_element_type=single)
    grad_inproj_bias = jnp.sum(d_proj.astype(single), (0, 1))
    d_attn_in = jnp.einsum("iqe,de->iqd", d_proj, inproj_weight, preferred_element_type=single)
    grad_attn_gain = jnp.sum(d_attn_in * xhat_one, (0, 1))
    grad_attn_shift = jnp.sum(d_attn_in, (0, 1))
    d_patches = d_mid + norm_back(d_attn_in, gain_one, xhat_one, rstd_one)
    d_patches = spread_image(d_patches.astype(low))
    small = (
        grad_attn_gain,
        grad_attn_shift,
        grad_inproj_bias,
        grad_outproj_bias,
        grad_mlp_gain,
        grad_mlp_shift,
        grad_expand_bias,
        grad_reduce_bias,
        grad_freqs.reshape(-1),
    )
    packed = lax.psum(jnp.concatenate(small), ("img", "band"))
    shares = lax.axis_size("img")
    mine = lax.axis_index("img")
    sums = []
    at = 0
    for piece in small:
        long = piece.shape[0]
        sums.append(packed[at : at + long])
        at += long
    freq_total = sums.pop().reshape(grad_freqs.shape)
    sums = [
        lax.dynamic_slice_in_dim(s, mine * (s.shape[0] // shares), s.shape[0] // shares)
        for s in sums
    ]
    return (
        block_out,
        d_patches,
        sums[0],
        sums[1],
        matrix_sum(grad_inproj_weight),
        sums[2],
        freq_total,
        matrix_sum(grad_outproj_weight),
        sums[3],
        sums[4],
        sums[5],
        matrix_sum(grad_expand_weight),
        sums[6],
        matrix_sum(grad_reduce_weight),
        sums[7],
    )


def solution(mesh):
    act = P("img", "band", None)
    row = P("img")
    mat = P("img", None)
    return jax.shard_map(
        local,
        mesh=mesh,
        in_specs=(act, P("img", "band"), P("img", None)) + (P(),) * 13 + (act,),
        out_specs=(act, act, row, row, mat, row, P(), mat, row, row, row, mat, row, mat, row),
        check_vma=False,
    )
```

profile of v0, /device:TPU:0, one launch (start us, length us, event | category | flops | bytes accessed | tf_op | source)
XLA Modules:
  0.0 651.7 jit_solution(12072034389343736507)
XLA Ops:
  65.4 7.4 %fusion.34 = f32[12,576,576]{1,2,0:T(8,128)} fusion(bf16[576,12,32]{0,2,1:T(8,128)(2,1)S(1)} %bitcast.128, bf16[576,12,32]{0,2,1:T(8,128)(2,1)S(1)} %bitcast.130, bf16[576,12,32]{0,2,1:T(8,128)(2,1)S(1)} %bitcast.126, bf16[576,12,32]{0,2,1:T(8,128)(2,1)S(1)} %bitcast.124), kind=kOutput, calls=%fused_computation.88 | convolution fusion | flops 513146880 | bytes 17694720 | tf_op jit(solution)/shard_map/iqhd,ikhd->ihqk/dot_general | solution.py:93
  72.7 22.2 %fusion.54 = (f32[12,576]{1,0:T(8,128)}, f32[12,576,576]{1,2,0:T(8,128)}) fusion(f32[12,576,576]{1,2,0:T(8,128)} %fusion.34, pred[576]{0:T(1024)(128)(4,1)} %broadcast_compare_fusion), kind=kOutput, calls=%fused_computation.138 | output fusion | flops 23888448 | bytes 31878720 | tf_op jit(solution)/shard_map/sub | solution.py:95
  94.9 8.4 %fusion.21 = bf16[12,64,576]{2,1,0:T(8,128)(2,1)S(1)} fusion(f32[1,576,3,12,64]{1,4,3,2,0:T(8,128)} %bitcast.122, f32[12,576,576]{1,2,0:T(8,128)} %get-tuple-element.113, f32[12,576]{1,0:T(8,128)} %get-tuple-element.112), kind=kOutput, calls=%fused_computation.63 | convolution fusion | flops 518012928 | bytes 19603456 | tf_op jit(solution)/shard_map/ihqk,ikhd->iqhd/dot_general | solution.py:98
  112.8 8.9 %multiply_convert_fusion.1 = (bf16[576,3072]{1,0:T(8,128)(2,1)}, f32[576,3072]{1,0:T(8,128)}) fusion(f32[3072]{0:T(1024)} %convert_element_type.313, bf16[768,3072]{1,0:T(8,128)(2,1)} %param.29, f32[576,768]{1,0:T(8,128)} %fusion.20, f32[768]{0:T(1024)} %convert_element_type.311, f32[768]{0:T(1024)} %convert_element_type.310, f32[576]{0:T(1024)S(1)} %add_rsqrt_fusion, ...), kind=kOutput, calls=%fused_computation.18 | convolution fusion | flops 2730737664 | bytes 17127936 | tf_op jit(solution)/shard_map/dot_general | solution.py:105
  123.2 9.2 %convert_reduce_fusion = (f32[3072]{0:T(1024)}, bf16[576,3072]{1,0:T(8,128)(2,1)S(1)}) fusion(f32[576,3072]{1,0:T(8,128)} %get-tuple-element.115, f32[3072]{0:T(1024)} %convert_element_type.313, bf16[576,768]{1,0:T(8,128)(2,1)S(1)} %fusion.19, bf16[3072,768]{1,0:T(8,128)(2,1)} %param.31), kind=kOutput, calls=%fused_computation.17 | convolution fusion | flops 2740909056 | bytes 16244736 | tf_op jit(solution)/shard_map/iqd,fd->iqf/dot_general | solution.py:117
  132.4 7.6 %multiply_reduce_fusion.1 = (f32[768]{0:T(1024)}, f32[576]{0:T(1024)S(1)}, f32[576]{0:T(1024)S(1)}, f32[768]{0:T(1024)}, f32[576,768]{1,0:T(8,128)S(1)}) fusion(f32[576,768]{1,0:T(8,128)S(1)} %copy-done.1, f32[576]{0:T(1024)S(1)} %copy-done.40, f32[576]{0:T(1024)S(1)} %copy-done.32, f32[768]{0:T(1024)S(1)} %copy-done.37, ...), kind=kOutput, calls=%fused_computation.46 | convolution fusion | flops 2721887744 | bytes 11814912 | tf_op jit(solution)/shard_map/iqf,df->iqd/dot_general | solution.py:121
  151.8 15.5 %multiply_reduce_fusion = (f32[12,576]{1,0:T(8,128)S(1)}, f32[12,576,576]{1,2,0:T(8,128)}) fusion(f32[12,576,576]{1,2,0:T(8,128)} %get-tuple-element.113, f32[12,576]{1,0:T(8,128)} %get-tuple-element.112, bf16[576,12,64]{0,2,1:T(8,128)(2,1)} %bitcast.144, f32[1,576,3,12,64]{1,4,3,2,0:T(8,128)} %bitcast.123), kind=kOutput, calls=%fused_computation.2 | convolution fusion | flops 521544960 | bytes 35654656 | tf_op jit(solution)/shard_map/iqhd,ikhd->ihqk/dot_general | solution.py:131
  167.3 12.5 %multiply_convert_fusion = bf16[12,576,576]{1,2,0:T(8,128)(2,1)S(1)} fusion(f32[12,576,576]{1,2,0:T(8,128)} %get-tuple-element.118, f32[12,576]{1,0:T(8,128)S(1)} %get-tuple-element.117, f32[12,576,576]{1,2,0:T(8,128)} %get-tuple-element.113, f32[12,576]{1,0:T(8,128)S(1)} %copy-done.27), kind=kLoop, calls=%fused_computation.1 | loop fusion | flops 15925248 | bytes 39868416 | tf_op jit(solution)/shard_map/convert_element_type | solution.py:133
  195.1 9.5 %fusion.24 = bf16[12,64,576]{2,1,0:T(8,128)(2,1)S(1)} fusion(bf16[576,12,64]{0,2,1:T(8,128)(2,1)S(1)} %bitcast.145, f32[12,576,576]{1,2,0:T(8,128)} %get-tuple-element.113, f32[12,576]{1,0:T(8,128)S(1)} %copy-done.28), kind=kOutput, calls=%fused_computation.64 | convolution fusion | flops 518012928 | bytes 17722368 | tf_op jit(solution)/shard_map/ihqk,iqhd->ikhd/dot_general | solution.py:130
  205.6 7.2 %convolution_convert_fusion = bf16[768,2304]{0,1:T(8,128)(2,1)} fusion(bf16[576,768]{0,1:T(8,128)(2,1)S(1)} %bitcast.146, bf16[576,768]{0,1:T(8,128)(2,1)S(1)} %bitcast.141, bf16[576,768]{0,1:T(8,128)(2,1)S(1)} %bitcast.138, f32[576,768]{1,0:T(8,128)S(1)} %copy-done.16, f32[768]{0:T(1024)S(1)} %copy-done.43, f32[768]{0:T(1024)S(1)} %copy-done.35), kind=kOutput, calls=%fused_computation.21 | convolution fusion | flops 2049490944 | bytes 7968768 | tf_op jit(solution)/shard_map/iqd,iqe->de/dot_general | solution.py:156
  213.0 8.3 %convolution_convert_fusion.1 = bf16[3072,768]{0,1:T(8,128)(2,1)} fusion(bf16[576,3072]{1,0:T(8,128)(2,1)} %get-tuple-element.114, bf16[576,768]{1,0:T(8,128)(2,1)} %copy-done.20), kind=kOutput, calls=%fused_computation.22 | convolution fusion | flops 2720268288 | bytes 9142272 | tf_op jit(solution)/shard_map/iqf,iqd->fd/dot_general | solution.py:115
  222.1 9.2 %convolution_convert_fusion.2 = bf16[768,3072]{1,0:T(8,128)(2,1)} fusion(bf16[576,3072]{1,0:T(8,128)(2,1)} %copy-done.50, f32[576,768]{1,0:T(8,128)} %fusion.20, f32[768]{0:T(1024)} %convert_element_type.311, f32[768]{0:T(1024)S(1)} %copy-done.38, f32[576]{0:T(1024)} %copy-done.39, f32[576]{0:T(1024)S(1)} %copy-done.33), kind=kOutput, calls=%fused_computation.23 | convolution fusion | flops 2722480128 | bytes 10037760 | tf_op jit(solution)/shard_map/iqd,iqf->df/dot_general | solution.py:119
  233.4 24.4 %reduce-scatter.15.cloned.1.call-done = bf16[768,576]{0,1:T(8,128)(2,1)} async-done(((bf16[768,2304]{0,1:T(8,128)(2,1)}), bf16[768,576]{0,1:T(8,128)(2,1)}) %reduce-scatter.15.cloned.1.call-update) | async-done | bytes 884752 | tf_op jit(solution)/shard_map/reduce_scatter | solution.py:31
  260.3 48.0 %reduce-scatter.23.cloned.1.call-done = bf16[3072,192]{0,1:T(8,128)(2,1)} async-done(((bf16[3072,768]{0,1:T(8,128)(2,1)}), bf16[3072,192]{0,1:T(8,128)(2,1)}) %reduce-scatter.23.cloned.1.call-update) | async-done | bytes 1179664 | tf_op jit(solution)/shard_map/reduce_scatter | solution.py:31
  320.8 8.0 %reduce.39 = bf16[576,768]{1,0:T(8,128)(2,1)} reduce(bf16[576,1,768]{2,1,0:T(2,128)(2,1)} %bitcast.134, bf16[]{:T(256)} %broadcast.353), dimensions={1}, to_apply=%bitcast.118.reduce_sub_computation | reduce | bytes 1769474
  348.6 19.5 %reduce-scatter.19.cloned.1.call-done = bf16[768,768]{1,0:T(8,128)(2,1)} async-done(((bf16[768,3072]{1,0:T(8,128)(2,1)}), bf16[768,768]{1,0:T(8,128)(2,1)}) %reduce-scatter.19.cloned.1.call-update) | async-done | bytes 1179664 | tf_op jit(solution)/shard_map/reduce_scatter | solution.py:31
  376.2 7.9 %reduce.40 = bf16[576,768]{1,0:T(8,128)(2,1)} reduce(bf16[576,1,768]{2,1,0:T(2,128)(2,1)} %bitcast.135, bf16[]{:T(256)} %broadcast.353), dimensions={1}, to_apply=%bitcast.117.reduce_sub_computation | reduce | bytes 1769474
  404.8 41.6 %psum.7 = f32[10752]{0:T(1024)} all-reduce(f32[10752]{0:T(1024)} %constant_dynamic-update-slice_fusion), channel_id=1, replica_groups=mesh['img'=8,'band'=4] {'img','band'}, use_global_device_ids=true, to_apply=%region_21.22 | all-reduce | flops 10752 | bytes 86016 | tf_op jit(solution)/shard_map/psum | solution.py:174
  472.2 7.9 %all_gather.13 = bf16[96,768]{0,1:T(8,128)(2,1)} all-gather(bf16[96,192]{0,1:T(8,128)(2,1)} %copy.89), channel_id=1, replica_groups=mesh['img'=8,'band'=4] {'band'}, dimensions={1}, use_global_device_ids=true | all-gather | bytes 184320 | tf_op jit(solution)/shard_map/all_gather | solution.py:33
  481.9 18.5 %reduce-scatter.25.cloned.1.call-done = bf16[96,576]{1,0:T(8,128)(2,1)} async-done(((bf16[768,576]{1,0:T(8,128)(2,1)}), bf16[96,576]{1,0:T(8,128)(2,1)}) %reduce-scatter.25.cloned.1.call-update) | async-done | bytes 110608
  514.9 53.6 %reduce-scatter.29.cloned.1.call-done = bf16[384,192]{1,0:T(8,128)(2,1)} async-done(((bf16[3072,192]{1,0:T(8,128)(2,1)}), bf16[384,192]{1,0:T(8,128)(2,1)}) %reduce-scatter.29.cloned.1.call-update) | async-done | bytes 147472
  570.2 8.4 %all_gather.15 = bf16[384,768]{0,1:T(8,128)(2,1)} all-gather(bf16[384,192]{0,1:T(8,128)(2,1)} %copy.91), channel_id=1, replica_groups=mesh['img'=8,'band'=4] {'band'}, dimensions={1}, use_global_device_ids=true | all-gather | bytes 737280 | tf_op jit(solution)/shard_map/all_gather | solution.py:33
  580.8 54.7 %reduce-scatter.21.cloned.1.call-done = bf16[96,768]{1,0:T(8,128)(2,1)} async-done(((bf16[768,768]{1,0:T(8,128)(2,1)}), bf16[96,768]{1,0:T(8,128)(2,1)}) %reduce-scatter.21.cloned.1.call-update) | async-done | bytes 147472 | tf_op jit(solution)/shard_map/reduce_scatter | solution.py:32
  635.5 7.7 %all_gather.14 = bf16[96,3072]{1,0:T(8,128)(2,1)S(1)} all-gather(bf16[96,768]{1,0:T(8,128)(2,1)} %reduce-scatter.21.cloned.1.call-done), channel_id=1, replica_groups=mesh['img'=8,'band'=4] {'band'}, dimensions={1}, use_global_device_ids=true | all-gather | bytes 737280 | tf_op jit(solution)/shard_map/all_gather | solution.py:33
  (235 shorter events, 210.3 us)
Async XLA Ops:
  7.2 38.6 %copy-start = (bf16[768,2304]{1,0:T(8,128)(2,1)S(1)}, bf16[768,2304]{1,0:T(8,128)(2,1)}, u32[]{:S(2)}) copy-start(bf16[768,2304]{1,0:T(8,128)(2,1)} %param.22) | copy-start | bytes 10616836
  8.6 8.0 %all-to-all-start = ((s32[4,1,144]{2,1,0:T(1,128)}), s32[4,1,144]{2,1,0:T(1,128)S(1)}, u32[]{:S(2)}, u32[]{:S(2)}) async-start(s32[4,1,144]{2,1,0:T(1,128)} %all_to_all.17), calls=%async_computation | async-start | bytes 8192 | tf_op jit(solution)/shard_map/all_to_all | solution.py:66
  16.7 17.0 %all-to-all-start.1 = ((bf16[4,144,768]{2,1,0:T(8,128)(2,1)}), bf16[4,144,768]{2,1,0:T(8,128)(2,1)}, u32[]{:S(2)}, u32[]{:S(2)}) async-start(bf16[4,144,768]{2,1,0:T(8,128)(2,1)} %param.17), calls=%async_computation.1 | async-start | bytes 1769472 | tf_op jit(solution)/shard_map/all_to_all | solution.py:66
  33.7 88.0 %all-to-all-start.3 = ((bf16[4,144,768]{2,1,0:T(8,128)(2,1)}), bf16[4,144,768]{2,1,0:T(8,128)(2,1)}, u32[]{:S(2)}, u32[]{:S(2)}) async-start(bf16[4,144,768]{2,1,0:T(8,128)(2,1)} %param.33), calls=%async_computation.3 | async-start | bytes 1769472 | tf_op jit(solution)/shard_map/all_to_all | solution.py:66
  37.9 193.4 %reduce-scatter.17.cloned.1.call-start = ((), (), s32[]{:S(2)}) async-start(), calls=%async_computation.14 | async-start | bytes 1474560 | tf_op jit(solution)/shard_map/reduce_scatter | solution.py:31
  151.8 15.5 %copy-start.27 = (f32[12,576]{1,0:T(8,128)S(1)}, f32[12,576]{1,0:T(8,128)}, u32[]{:S(2)}) copy-start(f32[12,576]{1,0:T(8,128)} %get-tuple-element.112) | copy-start | bytes 82948
  167.3 12.5 %copy-start.3 = (bf16[1,576,12,32]{1,3,2,0:T(8,128)(2,1)S(1)}, bf16[1,576,12,32]{1,3,2,0:T(8,128)(2,1)}, u32[]{:S(2)}) copy-start(bf16[1,576,12,32]{1,3,2,0:T(8,128)(2,1)} %copy-done.2) | copy-start | bytes 1327108
  167.3 12.6 %copy-start.5 = (bf16[1,576,12,32]{1,3,2,0:T(8,128)(2,1)S(1)}, bf16[1,576,12,32]{1,3,2,0:T(8,128)(2,1)}, u32[]{:S(2)}) copy-start(bf16[1,576,12,32]{1,3,2,0:T(8,128)(2,1)} %copy-done.4) | copy-start | bytes 1327108
  186.9 70.9 %reduce-scatter.15.cloned.1.call-start = ((), (), s32[]{:S(2)}) async-start(), calls=%async_computation.13 | async-start | bytes 4423680 | tf_op jit(solution)/shard_map/reduce_scatter | solution.py:31
  193.6 11.0 %copy-start.11 = (bf16[1,576,12,64]{1,3,2,0:T(8,128)(2,1)}, bf16[1,576,12,64]{1,3,2,0:T(8,128)(2,1)S(1)}, u32[]{:S(2)}) copy-start(bf16[1,576,12,64]{1,3,2,0:T(8,128)(2,1)S(1)} %maximum_convert_fusion) | copy-start | bytes 2654212
  195.1 10.5 %copy-start.16 = (f32[576,768]{1,0:T(8,128)S(1)}, f32[576,768]{1,0:T(8,128)}, u32[]{:S(2)}) copy-start(f32[576,768]{1,0:T(8,128)} %copy-done.15) | copy-start | bytes 5308420
  195.1 10.5 %copy-start.35 = (f32[768]{0:T(1024)S(1)}, f32[768]{0:T(1024)}, u32[]{:S(2)}) copy-start(f32[768]{0:T(1024)} %convert_element_type.296) | copy-start | bytes 9220
  195.1 10.4 %copy-start.43 = (f32[768]{0:T(1024)S(1)}, f32[768]{0:T(1024)}, u32[]{:S(2)}) copy-start(f32[768]{0:T(1024)} %convert_element_type.297) | copy-start | bytes 9220
  212.8 95.5 %reduce-scatter.23.cloned.1.call-start = ((), (), s32[]{:S(2)}) async-start(), calls=%async_computation.17 | async-start | bytes 5898240 | tf_op jit(solution)/shard_map/reduce_scatter | solution.py:31
  221.4 146.7 %reduce-scatter.19.cloned.1.call-start = ((), (), s32[]{:S(2)}) async-start(), calls=%async_computation.15 | async-start | bytes 5898240 | tf_op jit(solution)/shard_map/reduce_scatter | solution.py:31
  231.3 29.0 %copy-start.46 = (bf16[768]{0:T(1024)(128)(2,1)S(1)}, bf16[768]{0:T(1024)(128)(2,1)}, u32[]{:S(2)}) copy-start(bf16[768]{0:T(1024)(128)(2,1)} %param.32) | copy-start | bytes 4612
  231.3 239.4 %reduce-scatter.27.cloned.1.call-start = ((), (), s32[]{:S(2)}) async-start(), calls=%async_computation.19 | async-start | bytes 442368
  233.3 267.1 %reduce-scatter.25.cloned.1.call-start = ((), (), s32[]{:S(2)}) async-start(), calls=%async_computation.18 | async-start | bytes 1105920
  260.0 308.4 %reduce-scatter.29.cloned.1.call-start = ((), (), s32[]{:S(2)}) async-start(), calls=%async_computation.20 | async-start | bytes 1769472
  332.3 61.7 %all-to-all-start.2 = ((bf16[4,2,55296]{2,1,0:T(2,128)(2,1)}), bf16[4,2,55296]{2,1,0:T(2,128)(2,1)}, u32[]{:S(2)}, u32[]{:S(2)}) async-start(bf16[4,2,55296]{2,1,0:T(2,128)(2,1)} %reshape.788), calls=%async_computation.2 | async-start | bytes 1769472 | tf_op jit(solution)/shard_map/all_to_all | solution.py:69
  336.5 299.0 %reduce-scatter.21.cloned.1.call-start = ((), (), s32[]{:S(2)}) async-start(), calls=%async_computation.16 | async-start | bytes 1327104 | tf_op jit(solution)/shard_map/reduce_scatter | solution.py:32
  376.2 12.6 %copy-start.45 = (f32[768]{0:T(1024)S(1)}, f32[768]{0:T(1024)}, u32[]{:S(2)}) copy-start(f32[768]{0:T(1024)} %get-tuple-element.80) | copy-start | bytes 9220
  376.2 13.9 %copy-start.26 = (f32[576]{0:T(1024)S(1)}, f32[576]{0:T(1024)}, u32[]{:S(2)}) copy-start(f32[576]{0:T(1024)} %get-tuple-element.123) | copy-start | bytes 6916
  394.0 70.3 %all-to-all-start.4 = ((bf16[4,2,55296]{2,1,0:T(2,128)(2,1)}), bf16[4,2,55296]{2,1,0:T(2,128)(2,1)}, u32[]{:S(2)}, u32[]{:S(2)}) async-start(bf16[4,2,55296]{2,1,0:T(2,128)(2,1)} %reshape.790), calls=%async_computation.4 | async-start | bytes 1769472 | tf_op jit(solution)/shard_map/all_to_all | solution.py:69
  (40 other events, 176.9 us)
Sparse Core Ops, SparseCore 0:
  187.0 27.7 reduce-scatter.16
  217.4 40.3 reduce-scatter.14
  260.3 47.9 reduce-scatter.22
  310.7 57.2 reduce-scatter.18
  371.1 62.2 reduce-scatter.26
  437.2 63.1 reduce-scatter.24
  503.8 64.5 reduce-scatter.28
  571.9 63.6 reduce-scatter.20
where the time goes:
time: 658 us; the launch traced here: 652 us
  waiting for transfers between devices  220 us (33%)
  matrix products  125 us (19%)
  other arithmetic  99.8 us (15%)
  local copies, waits for them, and re-layouts  95.8 us (15%)
  blocking collectives  72.8 us (11%)
  starting transfers between devices  22.4 us (3%)
  between operations  15.3 us (2%)
    reduce_scatter x4, waiting for transfers between devices, matrix_sum(): low = lax.psum_scatter(low, 'band', scatter_dimension=1, tiled=True)  91.9 us
    unnamed x11, waiting for transfers between devices  72.2 us
    unnamed x127, local copies, waits for them, and re-layouts  57.3 us
    reduce_scatter x1, waiting for transfers between devices, matrix_sum(): low = lax.psum_scatter(low, 'img', scatter_dimension=0, tiled=True)  54.7 us
    psum x1, blocking collectives, local(): packed = lax.psum(jnp.concatenate(small), ('img', 'band'))  41.6 us
    all_gather x4, blocking collectives, matrix_sum(): low = lax.all_gather(low, 'band', axis=1, tiled=True)  31.2 us
    sub x1, other arithmetic, local(): expo = jnp.exp(masked - jnp.max(masked, -1, keepdims=True))  22.2 us
    unnamed x3, other arithmetic  16 us
  transfers between devices with their start and end apart: 13, of which 7 were waited for; matrix products, arithmetic and copies ran while one was open for 38% of the time, Pallas kernels for 0%

commit v1 on v0

--- a/solution.py
+++ b/solution.py
@@ -1,3 +1,4 @@
+import functools
 import jax
 import jax.numpy as jnp
 from jax import lax
@@ -8,6 +9,44 @@
 NEG = -1e30
 
 
+def begin_sources_all(inp, d_out):
+    v1 = list(inp.shape[1:])
+    v1[d_out] *= inp.shape[0]
+    val2 = jnp.moveaxis(inp, 0, d_out).reshape(v1)
+    return val2
+
+
+def map_the_bench(a0, comm_axis):
+    out_arr = jax.lax.axis_size(comm_axis)
+    upper = jax.lax.axis_index(comm_axis)
+    odd, side_arr = (out_arr, upper)
+    b_next, arr_next = (a0[None], 1)
+    while arr_next < odd:
+        arrivals = []
+        i0 = 0
+        while i0 < odd:
+            arrivals.append((i0, i0 ^ arr_next))
+            i0 += 1
+        value_now = jax.lax.ppermute(b_next, axis_name=comm_axis, perm=arrivals)
+        current_value = side_arr & arr_next == 0
+        b_next = jnp.concatenate(
+            [
+                jnp.where(current_value, b_next, value_now),
+                jnp.where(current_value, value_now, b_next),
+            ]
+        )
+        arr_next *= 2
+    return b_next
+
+
+def do_column_for(vals, load, out_dim):
+    met_up = begin_sources_all(map_the_bench(vals, load), out_dim)
+    return met_up
+
+
+answer_frame = functools.partial(do_column_for, load="band", out_dim=1)
+
+
 def norm_parts(values):
     center = values - jnp.mean(values, -1, keepdims=True)
     rstd = lax.rsqrt(jnp.mean(center * center, -1, keepdims=True) + EPS)
@@ -30,7 +69,7 @@
     low = grad.astype(jnp.bfloat16)
     low = lax.psum_scatter(low, "band", scatter_dimension=1, tiled=True)
     low = lax.psum_scatter(low, "img", scatter_dimension=0, tiled=True)
-    low = lax.all_gather(low, "band", axis=1, tiled=True)
+    low = answer_frame(low)
     return low.astype(jnp.float32)
 
 

time: 658 us -> 669 us (1.017)
  blocking collectives: 72.8 us -> 41.8 us
  waiting for transfers between devices: 220 us -> 248 us
  other arithmetic: 99.8 us -> 109 us
    all_gather x4 -> x0, blocking collectives: 31.2 us -> none  [matrix_sum(): low = lax.all_gather(low, 'band', axis=1, tiled=True)]
    unnamed x11, waiting for transfers between devices: 72.2 us -> 91.6 us
    ppermute x0 -> x8, waiting for transfers between devices: none -> 8.36 us  [map_the_bench(): value_now = jax.lax.ppermute(b_next, axis_name=comm_axis, perm=arrivals)]
    select_n x0 -> x8, other arithmetic: none -> 7.54 us  [map_the_bench(): jnp.where(current_value, b_next, value_now)]
    unnamed x127 -> x159, local copies, waits for them, and re-layouts: 57.3 us -> 60 us
    unnamed x3 -> x4, other arithmetic: 16 us -> 16.1 us
  transfers between devices with their start and end apart: 13 -> 21, of which waited for: 7 -> 10; matrix products, arithmetic and copies ran while one was open for 38% -> 38% of each run, Pallas kernels for 0% -> 0%
where the time goes in v1:
time: 669 us; the launch traced here: 662 us
  waiting for transfers between devices  248 us (37%)
  matrix products  124 us (19%)
  other arithmetic  109 us (16%)
  local copies, waits for them, and re-layouts  96.9 us (14%)
  blocking collectives  41.8 us (6%)
  starting transfers between devices  26.6 us (4%)
  between operations  15.5 us (2%)
    unnamed x11, waiting for transfers between devices  91.6 us
    reduce_scatter x4, waiting for transfers between devices, matrix_sum(): low = lax.psum_scatter(low, 'band', scatter_dimension=1, tiled=True)  86.3 us
    reduce_scatter x1, waiting for transfers between devices, matrix_sum(): low = lax.psum_scatter(low, 'img', scatter_dimension=0, tiled=True)  60.5 us
    unnamed x159, local copies, waits for them, and re-layouts  60 us
    psum x1, blocking collectives, local(): packed = lax.psum(jnp.concatenate(small), ('img', 'band'))  41.8 us
    sub x1, other arithmetic, local(): expo = jnp.exp(masked - jnp.max(masked, -1, keepdims=True))  22.3 us
    unnamed x4, other arithmetic  16.1 us
    dot_general x1, matrix products, local(): jnp.einsum('iqhd,ikhd->ihqk', d_mix, value_low, preferred_element_type=si...  15.5 us
  transfers between devices with their start and end apart: 21, of which 10 were waited for; matrix products, arithmetic and copies ran while one was open for 38% of the time, Pallas kernels for 0%

profile of v1, /device:TPU:0, one launch (start us, length us, event | category | flops | bytes accessed | tf_op | source)
XLA Modules:
  0.0 662.2 jit_solution(3951728900937166714)
XLA Ops:
  50.3 6.5 copy.70
  65.3 7.4 %fusion.34 = f32[12,576,576]{1,2,0:T(8,128)} fusion(bf16[576,12,32]{0,2,1:T(8,128)(2,1)S(1)} %bitcast.147, bf16[576,12,32]{0,2,1:T(8,128)(2,1)S(1)} %bitcast.149, bf16[576,12,32]{0,2,1:T(8,128)(2,1)S(1)} %bitcast.145, bf16[576,12,32]{0,2,1:T(8,128)(2,1)S(1)} %bitcast.143), kind=kOutput, calls=%fused_computation.89 | convolution fusion | flops 513146880 | bytes 17694720 | tf_op jit(solution)/shard_map/iqhd,ikhd->ihqk/dot_general | solution.py:132
  72.7 22.3 %fusion.54 = (f32[12,576]{1,0:T(8,128)}, f32[12,576,576]{1,2,0:T(8,128)}) fusion(f32[12,576,576]{1,2,0:T(8,128)} %fusion.34, pred[576]{0:T(1024)(128)(4,1)} %broadcast_compare_fusion), kind=kOutput, calls=%fused_computation.162 | output fusion | flops 23888448 | bytes 31878720 | tf_op jit(solution)/shard_map/sub | solution.py:134
  95.1 8.4 %fusion.21 = bf16[12,64,576]{2,1,0:T(8,128)(2,1)S(1)} fusion(f32[1,576,3,12,64]{1,4,3,2,0:T(8,128)} %bitcast.141, f32[12,576,576]{1,2,0:T(8,128)} %get-tuple-element.129, f32[12,576]{1,0:T(8,128)} %get-tuple-element.128), kind=kOutput, calls=%fused_computation.63 | convolution fusion | flops 518012928 | bytes 19603456 | tf_op jit(solution)/shard_map/ihqk,ikhd->iqhd/dot_general | solution.py:137
  113.0 8.9 %multiply_convert_fusion.1 = (bf16[576,3072]{1,0:T(8,128)(2,1)}, f32[576,3072]{1,0:T(8,128)}) fusion(f32[3072]{0:T(1024)} %convert_element_type.337, bf16[768,3072]{1,0:T(8,128)(2,1)} %param.29, f32[576,768]{1,0:T(8,128)} %fusion.20, f32[768]{0:T(1024)} %convert_element_type.335, f32[768]{0:T(1024)} %convert_element_type.334, f32[576]{0:T(1024)S(1)} %add_rsqrt_fusion, ...), kind=kOutput, calls=%fused_computation.18 | convolution fusion | flops 2730737664 | bytes 17127936 | tf_op jit(solution)/shard_map/dot_general | solution.py:144
  123.3 9.2 %convert_reduce_fusion = (f32[3072]{0:T(1024)}, bf16[576,3072]{1,0:T(8,128)(2,1)S(1)}) fusion(f32[576,3072]{1,0:T(8,128)} %get-tuple-element.131, f32[3072]{0:T(1024)} %convert_element_type.337, bf16[576,768]{1,0:T(8,128)(2,1)S(1)} %fusion.19, bf16[3072,768]{1,0:T(8,128)(2,1)} %param.31), kind=kOutput, calls=%fused_computation.17 | convolution fusion | flops 2740909056 | bytes 16244736 | tf_op jit(solution)/shard_map/iqd,fd->iqf/dot_general | solution.py:156
  132.5 7.6 %multiply_reduce_fusion.1 = (f32[768]{0:T(1024)}, f32[576]{0:T(1024)S(1)}, f32[576]{0:T(1024)S(1)}, f32[768]{0:T(1024)}, f32[576,768]{1,0:T(8,128)S(1)}) fusion(f32[576,768]{1,0:T(8,128)S(1)} %copy-done.3, f32[576]{0:T(1024)S(1)} %copy-done.55, f32[576]{0:T(1024)S(1)} %copy-done.45, f32[768]{0:T(1024)S(1)} %copy-done.52, ...), kind=kOutput, calls=%fused_computation.46 | convolution fusion | flops 2721887744 | bytes 11814912 | tf_op jit(solution)/shard_map/iqf,df->iqd/dot_general | solution.py:160
  152.0 15.5 %multiply_reduce_fusion = (f32[12,576]{1,0:T(8,128)S(1)}, f32[12,576,576]{1,2,0:T(8,128)}) fusion(f32[12,576,576]{1,2,0:T(8,128)} %get-tuple-element.129, f32[12,576]{1,0:T(8,128)} %get-tuple-element.128, bf16[576,12,64]{0,2,1:T(8,128)(2,1)} %bitcast.167, f32[1,576,3,12,64]{1,4,3,2,0:T(8,128)} %bitcast.142), kind=kOutput, calls=%fused_computation.2 | convolution fusion | flops 521544960 | bytes 35654656 | tf_op jit(solution)/shard_map/iqhd,ikhd->ihqk/dot_general | solution.py:170
  167.5 12.5 %multiply_convert_fusion = bf16[12,576,576]{1,2,0:T(8,128)(2,1)S(1)} fusion(f32[12,576,576]{1,2,0:T(8,128)} %get-tuple-element.134, f32[12,576]{1,0:T(8,128)S(1)} %get-tuple-element.133, f32[12,576,576]{1,2,0:T(8,128)} %get-tuple-element.129, f32[12,576]{1,0:T(8,128)S(1)} %copy-done.39), kind=kLoop, calls=%fused_computation.1 | loop fusion | flops 15925248 | bytes 39868416 | tf_op jit(solution)/shard_map/convert_element_type | solution.py:172
  187.1 6.6 multiply_subtract_fusion.1
  195.3 9.5 %fusion.24 = bf16[12,64,576]{2,1,0:T(8,128)(2,1)S(1)} fusion(bf16[576,12,64]{0,2,1:T(8,128)(2,1)S(1)} %bitcast.168, f32[12,576,576]{1,2,0:T(8,128)} %get-tuple-element.129, f32[12,576]{1,0:T(8,128)S(1)} %copy-done.40), kind=kOutput, calls=%fused_computation.64 | convolution fusion | flops 518012928 | bytes 17722368 | tf_op jit(solution)/shard_map/ihqk,iqhd->ikhd/dot_general | solution.py:169
  205.7 7.3 %convolution_convert_fusion = bf16[768,2304]{0,1:T(8,128)(2,1)} fusion(bf16[576,768]{0,1:T(8,128)(2,1)S(1)} %bitcast.169, bf16[576,768]{0,1:T(8,128)(2,1)S(1)} %bitcast.162, bf16[576,768]{0,1:T(8,128)(2,1)S(1)} %bitcast.159, f32[576,768]{1,0:T(8,128)S(1)} %copy-done.23, f32[768]{0:T(1024)S(1)} %copy-done.58, f32[768]{0:T(1024)S(1)} %copy-done.49), kind=kOutput, calls=%fused_computation.21 | convolution fusion | flops 2049490944 | bytes 7968768 | tf_op jit(solution)/shard_map/iqd,iqe->de/dot_general | solution.py:195
  213.3 8.3 %convolution_convert_fusion.1 = bf16[3072,768]{0,1:T(8,128)(2,1)} fusion(bf16[576,3072]{1,0:T(8,128)(2,1)} %get-tuple-element.130, bf16[576,768]{1,0:T(8,128)(2,1)} %copy-done.31), kind=kOutput, calls=%fused_computation.22 | convolution fusion | flops 2720268288 | bytes 9142272 | tf_op jit(solution)/shard_map/iqf,iqd->fd/dot_general | solution.py:154
  222.3 9.2 %convolution_convert_fusion.2 = bf16[768,3072]{1,0:T(8,128)(2,1)} fusion(bf16[576,3072]{1,0:T(8,128)(2,1)} %copy-done.66, f32[576,768]{1,0:T(8,128)} %fusion.20, f32[768]{0:T(1024)} %convert_element_type.335, f32[768]{0:T(1024)S(1)} %copy-done.53, f32[576]{0:T(1024)} %copy-done.54, f32[576]{0:T(1024)S(1)} %copy-done.46), kind=kOutput, calls=%fused_computation.23 | convolution fusion | flops 2722480128 | bytes 10037760 | tf_op jit(solution)/shard_map/iqd,iqf->df/dot_general | solution.py:158
  233.8 24.2 %reduce-scatter.15.cloned.1.call-done = bf16[768,576]{0,1:T(8,128)(2,1)} async-done(((bf16[768,2304]{0,1:T(8,128)(2,1)}), bf16[768,576]{0,1:T(8,128)(2,1)}) %reduce-scatter.15.cloned.1.call-update) | async-done | bytes 884752 | tf_op jit(solution)/shard_map/reduce_scatter | solution.py:70
  260.2 6.8 %fusion.27 = bf16[1,576,768]{2,1,0:T(8,128)(2,1)S(1)} fusion(f32[576,768]{1,0:T(8,128)} %fusion.20, bf16[576,3072]{1,0:T(8,128)(2,1)} %get-tuple-element.130, bf16[3072,768]{1,0:T(8,128)(2,1)} %param.31, f32[768]{0:T(1024)S(1)} %convert_element_type.339, f32[576]{0:T(1024)S(1)} %convert_element_type.314), kind=kOutput, calls=%fused_computation.67 | convolution fusion | flops 2719678464 | bytes 10917120 | tf_op jit(solution)/shard_map/dot_general | solution.py:149
  270.1 8.1 %reduce.39 = bf16[576,768]{1,0:T(8,128)(2,1)} reduce(bf16[576,1,768]{2,1,0:T(2,128)(2,1)} %bitcast.153, bf16[]{:T(256)} %broadcast.357), dimensions={1}, to_apply=%bitcast.137.reduce_sub_computation | reduce | bytes 1769474
  285.9 32.0 %reduce-scatter.23.cloned.1.call-done = bf16[3072,192]{0,1:T(8,128)(2,1)} async-done(((bf16[3072,768]{0,1:T(8,128)(2,1)}), bf16[3072,192]{0,1:T(8,128)(2,1)}) %reduce-scatter.23.cloned.1.call-update) | async-done | bytes 1179664 | tf_op jit(solution)/shard_map/reduce_scatter | solution.py:70
  338.2 30.0 %reduce-scatter.19.cloned.1.call-done = bf16[768,768]{1,0:T(8,128)(2,1)} async-done(((bf16[768,3072]{1,0:T(8,128)(2,1)}), bf16[768,768]{1,0:T(8,128)(2,1)}) %reduce-scatter.19.cloned.1.call-update) | async-done | bytes 1179664 | tf_op jit(solution)/shard_map/reduce_scatter | solution.py:70
  373.3 7.9 %reduce.40 = bf16[576,768]{1,0:T(8,128)(2,1)} reduce(bf16[576,1,768]{2,1,0:T(2,128)(2,1)} %bitcast.154, bf16[]{:T(256)} %broadcast.357), dimensions={1}, to_apply=%bitcast.136.reduce_sub_computation | reduce | bytes 1769474
  396.7 41.8 %psum.7 = f32[10752]{0:T(1024)} all-reduce(f32[10752]{0:T(1024)} %constant_dynamic-update-slice_fusion), channel_id=1, replica_groups=mesh['img'=8,'band'=4] {'img','band'}, use_global_device_ids=true, to_apply=%region_21.22 | all-reduce | flops 10752 | bytes 86016 | tf_op jit(solution)/shard_map/psum | solution.py:213
  465.7 34.8 %reduce-scatter.25.cloned.1.call-done = bf16[96,576]{1,0:T(8,128)(2,1)} async-done(((bf16[768,576]{1,0:T(8,128)(2,1)}), bf16[96,576]{1,0:T(8,128)(2,1)}) %reduce-scatter.25.cloned.1.call-update) | async-done | bytes 110608
  511.9 56.6 %reduce-scatter.29.cloned.1.call-done = bf16[384,192]{1,0:T(8,128)(2,1)} async-done(((bf16[3072,192]{1,0:T(8,128)(2,1)}), bf16[384,192]{1,0:T(8,128)(2,1)}) %reduce-scatter.29.cloned.1.call-update) | async-done | bytes 147472
  575.1 60.5 %reduce-scatter.21.cloned.1.call-done = bf16[96,768]{1,0:T(8,128)(2,1)} async-done(((bf16[768,768]{1,0:T(8,128)(2,1)}), bf16[96,768]{1,0:T(8,128)(2,1)}) %reduce-scatter.21.cloned.1.call-update) | async-done | bytes 147472 | tf_op jit(solution)/shard_map/reduce_scatter | solution.py:71
  (293 shorter events, 204.8 us)
Async XLA Ops:
  7.2 38.5 %copy-start = (bf16[768,2304]{1,0:T(8,128)(2,1)S(1)}, bf16[768,2304]{1,0:T(8,128)(2,1)}, u32[]{:S(2)}) copy-start(bf16[768,2304]{1,0:T(8,128)(2,1)} %param.22) | copy-start | bytes 10616836
  8.6 8.0 %all-to-all-start = ((s32[4,1,144]{2,1,0:T(1,128)}), s32[4,1,144]{2,1,0:T(1,128)S(1)}, u32[]{:S(2)}, u32[]{:S(2)}) async-start(s32[4,1,144]{2,1,0:T(1,128)} %all_to_all.17), calls=%async_computation | async-start | bytes 8192 | tf_op jit(solution)/shard_map/all_to_all | solution.py:105
  16.7 17.0 %all-to-all-start.1 = ((bf16[4,144,768]{2,1,0:T(8,128)(2,1)}), bf16[4,144,768]{2,1,0:T(8,128)(2,1)}, u32[]{:S(2)}, u32[]{:S(2)}) async-start(bf16[4,144,768]{2,1,0:T(8,128)(2,1)} %param.17), calls=%async_computation.1 | async-start | bytes 1769472 | tf_op jit(solution)/shard_map/all_to_all | solution.py:105
  33.7 88.2 %all-to-all-start.3 = ((bf16[4,144,768]{2,1,0:T(8,128)(2,1)}), bf16[4,144,768]{2,1,0:T(8,128)(2,1)}, u32[]{:S(2)}, u32[]{:S(2)}) async-start(bf16[4,144,768]{2,1,0:T(8,128)(2,1)} %param.33), calls=%async_computation.3 | async-start | bytes 1769472 | tf_op jit(solution)/shard_map/all_to_all | solution.py:105
  37.9 193.7 %reduce-scatter.17.cloned.1.call-start = ((), (), s32[]{:S(2)}) async-start(), calls=%async_computation.14 | async-start | bytes 1474560 | tf_op jit(solution)/shard_map/reduce_scatter | solution.py:70
  187.0 70.9 %reduce-scatter.15.cloned.1.call-start = ((), (), s32[]{:S(2)}) async-start(), calls=%async_computation.13 | async-start | bytes 4423680 | tf_op jit(solution)/shard_map/reduce_scatter | solution.py:70
  213.0 104.9 %reduce-scatter.23.cloned.1.call-start = ((), (), s32[]{:S(2)}) async-start(), calls=%async_computation.17 | async-start | bytes 5898240 | tf_op jit(solution)/shard_map/reduce_scatter | solution.py:70
  221.6 146.6 %reduce-scatter.19.cloned.1.call-start = ((), (), s32[]{:S(2)}) async-start(), calls=%async_computation.15 | async-start | bytes 5898240 | tf_op jit(solution)/shard_map/reduce_scatter | solution.py:70
  231.5 207.0 %reduce-scatter.27.cloned.1.call-start = ((), (), s32[]{:S(2)}) async-start(), calls=%async_computation.19 | async-start | bytes 442368
  233.5 267.1 %reduce-scatter.25.cloned.1.call-start = ((), (), s32[]{:S(2)}) async-start(), calls=%async_computation.18 | async-start | bytes 1105920
  281.6 104.3 %all-to-all-start.2 = ((bf16[4,2,55296]{2,1,0:T(2,128)(2,1)}), bf16[4,2,55296]{2,1,0:T(2,128)(2,1)}, u32[]{:S(2)}, u32[]{:S(2)}) async-start(bf16[4,2,55296]{2,1,0:T(2,128)(2,1)} %reshape.801), calls=%async_computation.2 | async-start | bytes 1769472 | tf_op jit(solution)/shard_map/all_to_all | solution.py:108
  285.9 35.0 %copy-start.35 = (f32[576]{0:T(1024)S(1)}, f32[576]{0:T(1024)}, u32[]{:S(2)}) copy-start(f32[576]{0:T(1024)} %copy-done.34) | copy-start | bytes 6916
  285.9 35.0 %copy-start.42 = (f32[576]{0:T(1024)S(1)}, f32[576]{0:T(1024)}, u32[]{:S(2)}) copy-start(f32[576]{0:T(1024)} %copy-done.41) | copy-start | bytes 6916
  285.9 282.6 %reduce-scatter.29.cloned.1.call-start = ((), (), s32[]{:S(2)}) async-start(), calls=%async_computation.20 | async-start | bytes 1769472
  320.5 315.0 %reduce-scatter.21.cloned.1.call-start = ((), (), s32[]{:S(2)}) async-start(), calls=%async_computation.16 | async-start | bytes 1327104 | tf_op jit(solution)/shard_map/reduce_scatter | solution.py:71
  386.0 72.0 %all-to-all-start.4 = ((bf16[4,2,55296]{2,1,0:T(2,128)(2,1)}), bf16[4,2,55296]{2,1,0:T(2,128)(2,1)}, u32[]{:S(2)}, u32[]{:S(2)}) async-start(bf16[4,2,55296]{2,1,0:T(2,128)(2,1)} %reshape.803), calls=%async_computation.4 | async-start | bytes 1769472 | tf_op jit(solution)/shard_map/all_to_all | solution.py:108
  440.0 24.3 %collective-permute-start.2 = (bf16[1,96,192]{1,2,0:T(8,128)(2,1)}, bf16[1,96,192]{1,2,0:T(8,128)(2,1)}, u32[]{:S(2)}, u32[]{:S(2)}) collective-permute-start(bf16[1,96,192]{1,2,0:T(8,128)(2,1)} %bitcast.176), channel_id=1, source_target_pairs={{0,1},{1,0},{2,3},{3,2},{4,5},{5,4},{6,7},{7,6},{8,9},{9,8},{10,11... | collective-permute-start | bytes 110600 | tf_op jit(solution)/shard_map/ppermute | solution.py:30
  502.2 2.4 collective-permute-start
  503.1 5.3 collective-permute-start.3
  507.0 63.2 %collective-permute-start.1 = (bf16[2,96,576]{1,2,0:T(8,128)(2,1)}, bf16[2,96,576]{1,2,0:T(8,128)(2,1)}, u32[]{:S(2)}, u32[]{:S(2)}) collective-permute-start(bf16[2,96,576]{1,2,0:T(8,128)(2,1)} %pad_maximum_fusion.9), channel_id=1, source_target_pairs={{0,2},{1,3},{2,0},{3,1},{4,6},{5,7},{6,4},{7,5},{8,10},{9,11},{10,... | collective-permute-start | bytes 663560 | tf_op jit(solution)/shard_map/ppermute | solution.py:30
  570.2 65.3 %collective-permute-start.6 = (bf16[1,384,192]{1,2,0:T(8,128)(2,1)}, bf16[1,384,192]{1,2,0:T(8,128)(2,1)}, u32[]{:S(2)}, u32[]{:S(2)}) collective-permute-start(bf16[1,384,192]{1,2,0:T(8,128)(2,1)} %bitcast.175), channel_id=1, source_target_pairs={{0,1},{1,0},{2,3},{3,2},{4,5},{5,4},{6,7},{7,6},{8,9},{9,8},{10,11... | collective-permute-start | bytes 442376 | tf_op jit(solution)/shard_map/ppermute | solution.py:30
  635.5 2.6 collective-permute-start.4
  636.6 9.9 %collective-permute-start.7 = (bf16[2,384,192]{1,2,0:T(8,128)(2,1)S(1)}, bf16[2,384,192]{1,2,0:T(8,128)(2,1)S(1)}, u32[]{:S(2)}, u32[]{:S(2)}) collective-permute-start(bf16[2,384,192]{1,2,0:T(8,128)(2,1)S(1)} %pad_maximum_fusion.11), channel_id=1, source_target_pairs={{0,2},{1,3},{2,0},{3,1},{4,6},{5,7},{6,4},{7,5},{8,10},{9,11},{10,... | collective-permute-start | bytes 884744 | tf_op jit(solution)/shard_map/ppermute | solution.py:30
  640.5 12.0 %collective-permute-start.5 = (bf16[2,96,768]{2,1,0:T(8,128)(2,1)}, bf16[2,96,768]{2,1,0:T(8,128)(2,1)}, u32[]{:S(2)}, u32[]{:S(2)}) collective-permute-start(bf16[2,96,768]{2,1,0:T(8,128)(2,1)} %pad_maximum_fusion.10), channel_id=1, source_target_pairs={{0,2},{1,3},{2,0},{3,1},{4,6},{5,7},{6,4},{7,5},{8,10},{9,11},{10,... | collective-permute-start | bytes 884744 | tf_op jit(solution)/shard_map/ppermute | solution.py:30
  (64 other events, 391.9 us)
Sparse Core Ops, SparseCore 0:
  187.1 27.8 reduce-scatter.16
  217.6 40.3 reduce-scatter.14
  260.5 57.4 reduce-scatter.22
  320.4 47.8 reduce-scatter.18
  371.3 62.2 reduce-scatter.26
  437.4 63.1 reduce-scatter.24
  504.0 64.4 reduce-scatter.28
  571.9 63.6 reduce-scatter.20
